TPU v7x, 256 devices: a whole 4x4x8 slice. The times are simulated.
256 devices in a mesh: seq: 16 (over z, core), head: 16 (over y, x).
Axes of the slice: x: 4, y: 4, z: 8, core: 2. Of those that a mesh axis runs over, the one named last changes fastest.
Arguments:
- queries: bfloat16 [6144, 16384], P('seq', 'head'), may hold values from -5 to 5
- keys: bfloat16 [6144, 1024], P('seq', 'head'), may hold values from -5 to 5
- values: bfloat16 [6144, 1024], P('seq', 'head'), may hold values from -6 to 6
- feat_q: bfloat16 [128, 128, 128], P('head'), may hold values from -0.5 to 0.5
- feat_k: bfloat16 [128, 128, 128], P('head'), may hold values from -0.5 to 0.5
Outputs:
- grad_feat_q: float32 [128, 128, 128], P('head')
- grad_feat_k: float32 [128, 128, 128], P('head')
All inputs are finite; a program needn't handle non-finite values.
Results may differ from a plain program's by a relative error of at most 0.02.
Values may be sent and summed in bfloat16 or wider, within the bound.
A program may use at most 128 MiB of HBM per device.

v0:
```python
import math
import jax
import jax.numpy as jnp
from jax import lax
from jax.sharding import PartitionSpec as P

HIGHEST_MODE = lax.Precision.HIGHEST
MASKED_SCORE = -1e30


def from_partner(block, axis, stride):
    count = lax.axis_size(axis)
    route = []
    for low in range(count):
        high = low | 1 << stride
        if high != low and high < count:
            route += [(low, high), (high, low)]
    return lax.ppermute(block, axis, route)


def in_one_piece(arrays, axis, dim, along):
    columns = [a.reshape(*a.shape[:along], -1) for a in arrays]
    both = jnp.concatenate(columns, axis=along)
    filled, at, done = (lax.all_gather(both, axis, axis=dim, tiled=True), 0, [])
    for a, column in zip(arrays, columns):
        piece = filled[..., at : at + column.shape[along]]
        done.append(piece.reshape(*piece.shape[:along], *a.shape[along:]))
        at += column.shape[along]
    return tuple(done)


def together(arrays, axis):
    vector, at, done = (jnp.concatenate([a.reshape(-1) for a in arrays]), 0, [])
    so_far = lax.psum(vector, axis)
    for a in arrays:
        done.append(so_far[at : at + a.size].reshape(a.shape))
        at += a.size
    return tuple(done)


def split_wide(entries):
    high = entries.astype(jnp.bfloat16)
    low = (entries - high.astype(jnp.float32)).astype(jnp.bfloat16)
    return (high, low)


def wide_left(form, wide, narrow):
    high, low = split_wide(wide)
    return jnp.einsum(form, high, narrow, preferred_element_type=jnp.float32) + jnp.einsum(
        form, low, narrow, preferred_element_type=jnp.float32
    )


def wide_right(form, narrow, wide):
    high, low = split_wide(wide)
    return jnp.einsum(form, narrow, high, preferred_element_type=jnp.float32) + jnp.einsum(
        form, narrow, low, preferred_element_type=jnp.float32
    )


def attend_block(
    running, query_half, query_pos, key_rows, value_rows, key_first, group_count, score_scale
):
    row_peak, row_total, summed = running
    half_rows = query_half.shape[0]
    key_count = key_rows.shape[0]
    head_dim = key_rows.shape[1] // group_count
    grouped = query_half.reshape(half_rows, group_count, -1, head_dim)
    key_heads = key_rows.reshape(key_count, group_count, head_dim)
    value_heads = value_rows.reshape(key_count, group_count, head_dim)
    scores = (
        jnp.einsum("rgjd,kgd->gjrk", grouped, key_heads, preferred_element_type=jnp.float32)
        * score_scale
    )
    scores = scores.reshape(row_peak.shape[0], half_rows, key_count)
    key_pos = key_first + jnp.arange(key_count, dtype=jnp.int32)
    allowed = (key_pos[None, :] <= query_pos[:, None])[None]
    new_peak = jnp.maximum(row_peak, jnp.max(jnp.where(allowed, scores, MASKED_SCORE), axis=-1))
    weights = jnp.exp(jnp.where(allowed, scores - new_peak[..., None], MASKED_SCORE))
    factor = jnp.exp(row_peak - new_peak)
    row_total = row_total * factor + jnp.sum(weights, axis=-1)
    rounded = weights.astype(jnp.bfloat16).reshape(group_count, -1, half_rows, key_count)
    mixture = jnp.einsum("gjrk,kgd->gjrd", rounded, value_heads, preferred_element_type=jnp.float32)
    summed = summed * factor[..., None] + mixture.reshape(summed.shape)
    return (new_peak, row_total, summed)


def body(queries, keys, values, feat_q, feat_k):
    row_count = queries.shape[0]
    heads_here = feat_q.shape[0]
    head_dim = feat_q.shape[1]
    seq_count = lax.axis_size("seq")
    seq_place = lax.axis_index("seq")
    head_place = lax.axis_index("head")
    key_value = jnp.stack((keys, values))
    partner = from_partner(key_value, "head", 0)
    upper_half = head_place // (1 << 0) % 2 == 1
    key_value = jnp.where(
        upper_half,
        jnp.concatenate((partner, key_value), axis=2),
        jnp.concatenate((key_value, partner), axis=2),
    )
    group_count = key_value.shape[2] // head_dim
    group_size = heads_here // group_count
    query_pos = seq_place * row_count + jnp.arange(row_count, dtype=jnp.int32)
    half_rows = row_count // 2
    query_halves = (queries[:half_rows], queries[half_rows:])
    pos_halves = (query_pos[:half_rows], query_pos[half_rows:])
    top_halves = (jnp.max(pos_halves[0]), jnp.max(pos_halves[1]))
    score_scale = head_dim ** (-0.5)
    start_half = (
        jnp.full((heads_here, half_rows), MASKED_SCORE, jnp.float32),
        jnp.zeros((heads_here, half_rows), jnp.float32),
        jnp.zeros((heads_here, half_rows, head_dim), jnp.float32),
    )
    shard_part = lax.all_gather(key_value, "seq", axis=1, tiled=True)
    part_rows = shard_part.shape[1]
    block_rows = math.gcd(part_rows, 512)

    def one_step(step_index, halves_state):
        offset = step_index * block_rows
        key_rows = lax.dynamic_slice_in_dim(shard_part[0], offset, block_rows, 0)
        value_rows = lax.dynamic_slice_in_dim(shard_part[1], offset, block_rows, 0)
        updated = []
        for half_index in range(2):

            def attend_half(current, half_index=half_index):
                return attend_block(
                    current,
                    query_halves[half_index],
                    pos_halves[half_index],
                    key_rows,
                    value_rows,
                    offset,
                    group_count,
                    score_scale,
                )

            def unchanged(current):
                return current

            updated.append(
                lax.cond(
                    top_halves[half_index] >= offset,
                    attend_half,
                    unchanged,
                    halves_state[half_index],
                )
            )
        return tuple(updated)

    finished = lax.fori_loop(0, part_rows // block_rows, one_step, (start_half, start_half))
    teacher_out = jnp.concatenate(
        [
            (finished[half_index][2] / finished[half_index][1][..., None]).astype(jnp.bfloat16)
            for half_index in range(2)
        ],
        axis=1,
    )
    key_local = key_value[0].reshape(row_count, group_count, head_dim)
    value_local = key_value[1].reshape(row_count, group_count, head_dim)
    query_local = queries.reshape(row_count, heads_here, head_dim)
    query_pre = jnp.einsum("rhd,hdf->hrf", query_local, feat_q, preferred_element_type=jnp.float32)
    key_pre = jnp.einsum(
        "rgd,gjdf->gjrf",
        key_local,
        feat_k.reshape(group_count, group_size, head_dim, -1),
        preferred_element_type=jnp.float32,
    ).reshape(heads_here, row_count, -1)
    feat_count = query_pre.shape[-1]
    query_feat = jax.nn.softplus(query_pre).astype(jnp.bfloat16)
    key_feat = jax.nn.softplus(key_pre).astype(jnp.bfloat16)
    block_state = jnp.einsum(
        "gjrf,rgd->gjfd",
        key_feat.reshape(group_count, group_size, row_count, -1),
        value_local,
        preferred_element_type=jnp.float32,
    ).reshape(heads_here, feat_count, head_dim)
    block_norm = jnp.sum(key_feat, axis=1, dtype=jnp.float32)
    zero_pair = (jnp.zeros_like(block_state), jnp.zeros_like(block_norm))
    take_shard_part = tuple(
        (
            part.astype(jnp.float32)
            for part in in_one_piece(
                (block_state[None].astype(jnp.bfloat16), block_norm[None].astype(jnp.bfloat16)),
                "seq",
                0,
                3,
            )
        )
    )
    part_count = take_shard_part[0].shape[0]
    chosen = jnp.arange(part_count, dtype=jnp.int32) < seq_place
    before_state = zero_pair[0] + jnp.sum(
        jnp.where(chosen[:, None, None, None], take_shard_part[0], 0.0), axis=0
    )
    before_norm = zero_pair[1] + jnp.sum(
        jnp.where(chosen[:, None, None], take_shard_part[1], 0.0), axis=0
    )
    causal = jnp.arange(row_count)[:, None] >= jnp.arange(row_count)[None, :]
    affinity = jnp.einsum("hrf,hsf->hrs", query_feat, key_feat, preferred_element_type=jnp.float32)
    masked = jnp.where(causal[None], affinity, 0.0)
    local_mix = jnp.einsum(
        "gjrs,sgd->gjrd",
        masked.astype(jnp.bfloat16).reshape(group_count, group_size, row_count, row_count),
        value_local,
        preferred_element_type=jnp.float32,
    ).reshape(heads_here, row_count, head_dim)
    numerator = wide_right("hrf,hfd->hrd", query_feat, before_state) + local_mix
    denominator = wide_right("hrf,hf->hr", query_feat, before_norm) + jnp.sum(masked, axis=-1)
    student = numerator / denominator[..., None]
    total_tokens = row_count * seq_count
    grad_out = 2.0 * (student - teacher_out.astype(jnp.float32)) / total_tokens
    grad_numer = grad_out / denominator[..., None]
    grad_denom = -jnp.sum(grad_out * student, axis=-1) / denominator
    back_state = wide_right("hrf,hrd->hfd", query_feat, grad_numer)
    back_norm = wide_right("hrf,hr->hf", query_feat, grad_denom)

    def take_upper(running, shard_part):
        part_count = shard_part[0].shape[0]
        chosen = jnp.arange(part_count, dtype=jnp.int32) > seq_place
        return (
            running[0]
            + jnp.sum(jnp.where(chosen[:, None, None, None], shard_part[0], 0.0), axis=0),
            running[1] + jnp.sum(jnp.where(chosen[:, None, None], shard_part[1], 0.0), axis=0),
        )

    after_state, after_norm = take_upper(
        zero_pair,
        (
            lax.all_gather(back_state[None].astype(jnp.bfloat16), "seq", axis=0, tiled=True).astype(
                jnp.float32
            ),
            lax.all_gather(back_norm[None].astype(jnp.bfloat16), "seq", axis=0, tiled=True).astype(
                jnp.float32
            ),
        ),
    )
    grad_aff = wide_left(
        "gjrd,sgd->gjrs",
        grad_numer.reshape(group_count, group_size, row_count, head_dim),
        value_local,
    ).reshape(heads_here, row_count, row_count)
    grad_aff = jnp.where(causal[None], grad_aff + grad_denom[..., None], 0.0)
    grad_qfeat = (
        jnp.einsum("hrd,hfd->hrf", grad_numer, before_state, precision=HIGHEST_MODE)
        + grad_denom[..., None] * before_norm[:, None, :]
        + wide_left("hrs,hsf->hrf", grad_aff, key_feat)
    )
    grad_kfeat = (
        wide_right(
            "sgd,gjfd->gjsf",
            value_local,
            after_state.reshape(group_count, group_size, feat_count, head_dim),
        ).reshape(heads_here, row_count, feat_count)
        + after_norm[:, None, :]
        + wide_left("hrs,hrf->hsf", grad_aff, query_feat)
    )
    grad_wq = wide_right("rhd,hrf->hdf", query_local, grad_qfeat * jax.nn.sigmoid(query_pre))
    grad_wk = wide_right(
        "rgd,gjrf->gjdf",
        key_local,
        (grad_kfeat * jax.nn.sigmoid(key_pre)).reshape(
            group_count, group_size, row_count, feat_count
        ),
    ).reshape(heads_here, head_dim, feat_count)
    return tuple(
        (
            part.astype(jnp.float32)
            for part in together(
                (grad_wq.astype(jnp.bfloat16), grad_wk.astype(jnp.bfloat16)), "seq"
            )
        )
    )


def solution(mesh):
    return jax.shard_map(
        body,
        mesh=mesh,
        in_specs=(
            P("seq", "head"),
            P("seq", "head"),
            P("seq", "head"),
            P("head", None, None),
            P("head", None, None),
        ),
        out_specs=(P("head", None, None), P("head", None, None)),
        check_vma=False,
    )
```

profile of v0, /device:TPU:1, one launch (start us, length us, event | category | flops | bytes accessed | tf_op | source)
XLA Modules:
  0.0 392.3 jit_solution(10411164082974506304)
XLA Ops:
  7.2 1.0 copy.115
  8.2 1.0 copy.116
  9.3 2.1 collective-permute-start
  11.4 3.4 collective-permute-done
  14.7 0.9 maximum_select_fusion
  17.0 0.9 select_convert_fusion.2
  18.1 1.1 fusion.123
  19.3 1.0 fusion.71
  21.4 2.2 select_reduce_fusion.1
  23.7 38.1 %all-gather.8.cloned.1.call-done = bf16[2,6144,128]{2,1,0:T(8,128)(2,1)} async-done(((bf16[2,384,128]{2,1,0:T(8,128)(2,1)}), bf16[2,6144,128]{2,1,0:T(8,128)(2,1)}) %all-gather.8.cloned.1.call-update) | async-done | bytes 3145744 | tf_op jit(solution)/shard_map/all_gather | solution.py:116
  61.9 1.0 broadcast_in_dim.136
  62.8 56.6 %while.23 = (s32[]{:T(128)}, f32[8,192]{1,0:T(8,128)S(1)}, f32[8,192]{1,0:T(8,128)S(1)}, f32[8,192,128]{2,1,0:T(8,128)}, f32[8,192]{1,0:T(8,128)S(1)}, /*index=5...) while((s32[]{:T(128)}, f32[8,192]{1,0:T(8,128)S(1)}, ...), condition=%wide.region_15.16_spmd, body=%wide.region_6.15_spmd.sunk | while | flops 823598080 | bytes 37431328 | solution.py:152
  64.0 2.1 fusion.153
  66.2 4.4 %conditional.4 = ((f32[8,192]{1,0:T(8,128)S(1)}, f32[8,192]{1,0:T(8,128)S(1)}, f32[8,192,128]{2,1,0:T(8,128)})) conditional(s32[]{:T(128)} %convert_element_type.400, (f32[8,192]{1,0:T(8,128)S(1)}, f32[8,192]{1,0:T(8,128)S(1)}, f32[8,192,128]{2,1,0:T(8,128)}) %tuple.74, (s32[]{:T(128)}, s32[192]{0:T(256)S(1)}, bf16[192,1024]{1,0:T(8,128)(2,1)S(1)}, ...), branch_computations={%region_7.7_spmd, %region_8.10_spmd} | conditional | flops 411799040 | bytes 18453340 | solution.py:143
  67.1 1.1 fusion.3
  68.2 1.5 fusion.14
  69.7 0.9 copy-done.13
  70.6 3.5 conditional.5
  71.5 1.1 fusion.27
  72.6 1.5 fusion.38
  75.3 2.1 fusion.153
  77.4 4.4 %conditional.4 = ((f32[8,192]{1,0:T(8,128)S(1)}, f32[8,192]{1,0:T(8,128)S(1)}, f32[8,192,128]{2,1,0:T(8,128)})) conditional(s32[]{:T(128)} %convert_element_type.400, (f32[8,192]{1,0:T(8,128)S(1)}, f32[8,192]{1,0:T(8,128)S(1)}, f32[8,192,128]{2,1,0:T(8,128)}) %tuple.74, (s32[]{:T(128)}, s32[192]{0:T(256)S(1)}, bf16[192,1024]{1,0:T(8,128)(2,1)S(1)}, ...), branch_computations={%region_7.7_spmd, %region_8.10_spmd} | conditional | flops 411799040 | bytes 18453340 | solution.py:143
  78.4 1.1 fusion.3
  79.5 1.4 fusion.14
  81.0 0.9 copy-done.13
  81.9 3.5 conditional.5
  82.8 1.1 fusion.27
  83.9 1.5 fusion.38
  86.6 2.1 fusion.153
  90.0 2.2 fusion.153
  93.5 2.1 fusion.153
  96.9 2.1 fusion.153
  100.3 2.1 fusion.153
  103.7 2.1 fusion.153
  107.1 2.1 fusion.153
  110.5 2.1 fusion.153
  113.9 2.1 fusion.153
  117.3 2.1 fusion.153
  119.5 0.9 copy-done.11
  120.3 1.5 copy.125
  121.8 2.5 copy.124
  124.3 2.4 divide_convert_fusion
  126.7 4.6 %slice.72 = bf16[16,8,128,128]{2,1,3,0:T(8,128)(2,1)} slice(bf16[16,8,128,129]{2,1,3,0:T(8,128)(2,1)} %all-gather.6.cloned.1.call-done), slice={[0:16], [0:8], [0:128], [0:128]} | slice | bytes 8388608 | tf_op jit(solution)/shard_map/slice | solution.py:26
  131.2 6.7 %copy.186 = bf16[16,8,128,128]{3,2,1,0:T(8,128)(2,1)} copy(bf16[16,8,128,128]{2,1,3,0:T(8,128)(2,1)} %slice.72) | data formatting | bytes 8388608
  137.9 3.2 select_reduce_fusion
  142.3 1.1 fusion.100
  144.2 1.1 multiply_reduce_fusion
  145.8 1.2 fusion.69
  147.3 2.8 fusion.128
  150.8 0.9 add_select_fusion
  152.0 0.9 fusion.115
  152.9 1.2 copy-done.2
  154.5 1.7 divide_multiply_fusion
  157.1 0.8 copy.138
  158.5 91.9 %all-gather.1 = bf16[128,128]{1,0:T(8,128)(2,1)S(1)} all-gather(bf16[8,128]{1,0:T(8,128)(2,1)S(1)} %add_convert_fusion), channel_id=3, replica_groups=mesh['seq'=16,'head'=16] {'seq'}, dimensions={0}, use_global_device_ids=true | all-gather | bytes 34816 | tf_op jit(solution)/shard_map/all_gather | solution.py:234
  250.5 4.7 %fusion.117 = f32[8,384,128]{2,1,0:T(8,128)S(1)} fusion(bf16[8,384,128]{2,1,0:T(8,128)(2,1)S(1)} %select_convert_fusion.2, f32[8,384,384]{1,2,0:T(8,128)} %copy-done.2), kind=kOutput, calls=%fused_computation.179 | convolution fusion | flops 306708480 | bytes 7077888 | tf_op jit(solution)/shard_map/hrs,hrf->hsf/dot_general | solution.py:49
  255.2 1.9 fusion.113
  257.2 7.9 %all-gather.10.cloned.1.call-done = bf16[128,128,128]{2,1,0:T(8,128)(2,1)} async-done(((bf16[8,128,128]{2,1,0:T(8,128)(2,1)}), bf16[128,128,128]{2,1,0:T(8,128)(2,1)}) %all-gather.10.cloned.1.call-update) | async-done | bytes 4194320 | tf_op jit(solution)/shard_map/all_gather | solution.py:231
  265.1 3.2 fusion.48
  268.8 1.0 copy-done.7
  269.9 2.1 fusion.55
  274.2 108.8 %all-reduce.2.cloned.1.call-done = bf16[262144]{0:T(1024)(128)(2,1)} async-done(((bf16[262144]{0:T(1024)(128)(2,1)}), bf16[262144]{0:T(1024)(128)(2,1)}) %all-reduce.2.cloned.1.call-update) | async-done | bytes 524304 | tf_op jit(solution)/shard_map/psum | solution.py:34
  383.0 1.1 fusion.127
  384.1 0.8 convert.7
  (149 shorter events, 16.1 us)
Async XLA Ops:
  7.2 10.8 %copy-start = (bf16[8,128,128]{2,1,0:T(8,128)(2,1)S(1)}, bf16[8,128,128]{2,1,0:T(8,128)(2,1)}, u32[]{:S(2)}) copy-start(bf16[8,128,128]{2,1,0:T(8,128)(2,1)} %param.15) | copy-start | bytes 786436
  7.2 9.3 %copy-start.5 = (bf16[384,1024]{1,0:T(8,128)(2,1)S(1)}, bf16[384,1024]{1,0:T(8,128)(2,1)}, u32[]{:S(2)}) copy-start(bf16[384,1024]{1,0:T(8,128)(2,1)} %param.11) | copy-start | bytes 2359300
  7.2 54.6 %all-gather.8.cloned.1.call-start = ((), (), s32[]{:S(2)}) async-start(), calls=%async_computation.1 | async-start | bytes 3342336 | tf_op jit(solution)/shard_map/all_gather | solution.py:116
  8.2 8.3 %copy-start.18 = (bf16[8,128,128]{2,1,0:T(8,128)(2,1)S(1)}, bf16[8,128,128]{2,1,0:T(8,128)(2,1)}, u32[]{:S(2)}) copy-start(bf16[8,128,128]{2,1,0:T(8,128)(2,1)} %param.14) | copy-start | bytes 786436
  9.3 5.5 %collective-permute-start = (bf16[2,384,64]{2,1,0:T(8,128)(2,1)S(1)}, bf16[2,384,64]{2,1,0:T(8,128)(2,1)S(1)}, u32[]{:S(2)}, u32[]{:S(2)}) collective-permute-start(bf16[2,384,64]{2,1,0:T(8,128)(2,1)S(1)} %pad_maximum_fusion.3), channel_id=1, source_target_pairs={{0,1},{1,0},{2,3},{3,2},{4,5},{5,4},{6,7},{7,6},{8,9},{9,8},{10,11... | collective-permute-start | bytes 294920 | tf_op jit(solution)/shard_map/ppermute | solution.py:18
  15.7 111.0 %all-gather.6.cloned.1.call-start = ((), (), s32[]{:S(2)}) async-start(), calls=%async_computation | async-start | bytes 4491264 | tf_op jit(solution)/shard_map/all_gather | solution.py:24
  17.0 2.2 copy-start.3
  17.0 1.1 copy-start.8
  19.2 1.2 copy-start.14
  19.2 2.2 copy-start.9
  21.2 243.9 %all-gather.10.cloned.1.call-start = ((), (), s32[]{:S(2)}) async-start(), calls=%async_computation.3 | async-start | bytes 4456448 | tf_op jit(solution)/shard_map/all_gather | solution.py:231
  67.1 1.1 copy-start.12
  69.7 0.9 copy-start.13
  78.4 1.2 copy-start.12
  81.0 0.9 copy-start.13
  119.5 0.9 copy-start.11
  141.8 2.4 copy-start.19
  142.2 1.9 copy-start.16
  142.3 1.9 copy-start.17
  147.0 236.0 %all-reduce.2.cloned.1.call-start = ((), (), s32[]{:S(2)}) async-start(), calls=%async_computation.2 | async-start | bytes 1048576 | tf_op jit(solution)/shard_map/psum | solution.py:34
  150.8 1.1 copy-start.10
  152.0 2.1 copy-start.2
  152.0 2.5 copy-start.4
  154.5 1.7 copy-start.6
  156.2 99.0 %slice-start = ((s8[4718592]{0:T(1024)(128)(4,1)}), s8[524288]{0:T(1024)(128)(4,1)S(1)}, s32[]{:S(2)}) async-start(s8[4718592]{0:T(1024)(128)(4,1)} %bitcast.271), calls=%async_computation.4 | async-start | bytes 1048576
  158.2 97.0 %slice-start.1 = ((s8[4718592]{0:T(1024)(128)(4,1)}), s8[4194304]{0:T(1024)(128)(4,1)S(1)}, s32[]{:S(2)}) async-start(s8[4718592]{0:T(1024)(128)(4,1)} %bitcast.271), calls=%async_computation.5 | async-start | bytes 8388608
  268.5 1.4 copy-start.7
  272.4 1.0 copy-start.15
  274.2 111.6 %copy-start.1 = (bf16[8,128,128]{2,1,0:T(8,128)(2,1)S(1)}, bf16[8,128,128]{2,1,0:T(8,128)(2,1)}, u32[]{:S(2)}) copy-start(bf16[8,128,128]{2,1,0:T(8,128)(2,1)} %param.15) | copy-start | bytes 786436
Sparse Core Ops, SparseCore 0:
  15.8 45.9 all-gather.7
  63.7 40.6 all-gather.5
  147.1 117.8 all-gather.9
  274.3 108.6 all-reduce.1
where the time goes:
time: 394 us; the launch traced here: 392 us
  waiting for transfers between devices  158 us (40%)
  blocking collectives  91.9 us (23%)
  local copies, waits for them, and re-layouts  53.3 us (14%)
  matrix products  36.4 us (9%)
  other arithmetic  20.1 us (5%)
  loops' own time  15.4 us (4%)
  between operations  14.2 us (4%)
    psum x1, waiting for transfers between devices, together(): so_far = lax.psum(vector, axis)  109 us
    all_gather x1, blocking collectives, body(): lax.all_gather(back_norm[None].astype(jnp.bfloat16), 'seq', axis=0, tiled...  91.9 us
    all_gather x1, waiting for transfers between devices, body(): shard_part = lax.all_gather(key_value, 'seq', axis=1, tiled=True)  38.1 us
    slice x12, local copies, waits for them, and re-layouts, one_step(): value_rows = lax.dynamic_slice_in_dim(shard_part[1], offset, block_rows, 0)  25.2 us
    another operation x1, loops' own time, body(): lax.fori_loop(0, part_rows // block_rows, one_step, (start_half, start_ha...  14.8 us
    unnamed x45, local copies, waits for them, and re-layouts  13.5 us
  transfers between devices with their start and end apart: 5, of which 4 were waited for; matrix products, arithmetic and copies ran while one was open for 18% of the time, Pallas kernels for 0%

commit v1 on v0

--- a/solution.py
+++ b/solution.py
@@ -30,8 +30,12 @@
 
 
 def together(arrays, axis):
+
+    def cut_copies(mat, peer_axis):
+        return jnp.sum(lax.all_gather(mat, peer_axis), axis=0)
+
     vector, at, done = (jnp.concatenate([a.reshape(-1) for a in arrays]), 0, [])
-    so_far = lax.psum(vector, axis)
+    so_far = cut_copies(vector, axis)
     for a in arrays:
         done.append(so_far[at : at + a.size].reshape(a.shape))
         at += a.size

time: 394 us -> 358 us (0.909)
  waiting for transfers between devices: 158 us -> 103 us
  other arithmetic: 20.1 us -> 32.1 us
  local copies, waits for them, and re-layouts: 53.3 us -> 59.9 us
    psum x1 -> x0, waiting for transfers between devices: 109 us -> none  [together(): so_far = lax.psum(vector, axis)]
    all_gather x0 -> x1, waiting for transfers between devices: none -> 54.6 us  [cut_copies(): return jnp.sum(lax.all_gather(mat, peer_axis), axis=0)]
    reduce_sum x0 -> x1, other arithmetic: none -> 11.9 us  [cut_copies(): return jnp.sum(lax.all_gather(mat, peer_axis), axis=0)]
    all_gather x0 -> x1, local copies, waits for them, and re-layouts: none -> 7.63 us  [cut_copies(): return jnp.sum(lax.all_gather(mat, peer_axis), axis=0)]
  transfers between devices with their start and end apart: 5 -> 5, of which waited for: 4 -> 4; matrix products, arithmetic and copies ran while one was open for 18% -> 20% of each run, Pallas kernels for 0% -> 0%
where the time goes in v1:
time: 358 us; the launch traced here: 357 us
  waiting for transfers between devices  103 us (29%)
  blocking collectives  92.6 us (26%)
  local copies, waits for them, and re-layouts  59.9 us (17%)
  matrix products  36.4 us (10%)
  other arithmetic  32.1 us (9%)
  loops' own time  15.4 us (4%)
  between operations  14.2 us (4%)
    all_gather x1, blocking collectives, body(): lax.all_gather(back_norm[None].astype(jnp.bfloat16), 'seq', axis=0, tiled...  92.6 us
    all_gather x1, waiting for transfers between devices, cut_copies(): return jnp.sum(lax.all_gather(mat, peer_axis), axis=0)  54.6 us
    all_gather x1, waiting for transfers between devices, body(): shard_part = lax.all_gather(key_value, 'seq', axis=1, tiled=True)  38.1 us
    slice x12, local copies, waits for them, and re-layouts, one_step(): value_rows = lax.dynamic_slice_in_dim(shard_part[1], offset, block_rows, 0)  25.2 us
    another operation x1, loops' own time, body(): lax.fori_loop(0, part_rows // block_rows, one_step, (start_half, start_ha...  14.8 us
    unnamed x45, local copies, waits for them, and re-layouts  13.5 us
    reduce_sum x1, other arithmetic, cut_copies(): return jnp.sum(lax.all_gather(mat, peer_axis), axis=0)  11.9 us
    all_gather x1, local copies, waits for them, and re-layouts, cut_copies(): return jnp.sum(lax.all_gather(mat, peer_axis), axis=0)  7.63 us
  transfers between devices with their start and end apart: 5, of which 4 were waited for; matrix products, arithmetic and copies ran while one was open for 20% of the time, Pallas kernels for 0%

profile of v1, /device:TPU:1, one launch (start us, length us, event | category | flops | bytes accessed | tf_op | source)
XLA Modules:
  0.0 356.6 jit_solution(12838883534251940371)
XLA Ops:
  7.2 1.0 copy.154
  8.2 1.0 copy.155
  9.3 2.1 collective-permute-start
  11.4 3.4 collective-permute-done
  14.7 0.9 maximum_select_fusion
  17.0 0.9 select_convert_fusion.2
  18.1 1.1 fusion.123
  19.3 1.0 fusion.71
  21.4 2.2 select_reduce_fusion.1
  23.7 38.1 %all-gather.10.cloned.1.call-done = bf16[2,6144,128]{2,1,0:T(8,128)(2,1)} async-done(((bf16[2,384,128]{2,1,0:T(8,128)(2,1)}), bf16[2,6144,128]{2,1,0:T(8,128)(2,1)}) %all-gather.10.cloned.1.call-update) | async-done | bytes 3145744 | tf_op jit(solution)/shard_map/all_gather | solution.py:120
  61.9 1.0 broadcast_in_dim.136
  62.8 56.6 %while.23 = (s32[]{:T(128)}, f32[8,192]{1,0:T(8,128)S(1)}, f32[8,192]{1,0:T(8,128)S(1)}, f32[8,192,128]{2,1,0:T(8,128)}, f32[8,192]{1,0:T(8,128)S(1)}, /*index=5...) while((s32[]{:T(128)}, f32[8,192]{1,0:T(8,128)S(1)}, ...), condition=%wide.region_15.16_spmd, body=%wide.region_6.15_spmd.sunk | while | flops 823598080 | bytes 37431328 | solution.py:156
  64.0 2.1 fusion.153
  66.2 4.4 %conditional.4 = ((f32[8,192]{1,0:T(8,128)S(1)}, f32[8,192]{1,0:T(8,128)S(1)}, f32[8,192,128]{2,1,0:T(8,128)})) conditional(s32[]{:T(128)} %convert_element_type.402, (f32[8,192]{1,0:T(8,128)S(1)}, f32[8,192]{1,0:T(8,128)S(1)}, f32[8,192,128]{2,1,0:T(8,128)}) %tuple.74, (s32[]{:T(128)}, s32[192]{0:T(256)S(1)}, bf16[192,1024]{1,0:T(8,128)(2,1)S(1)}, ...), branch_computations={%region_7.7_spmd, %region_8.10_spmd} | conditional | flops 411799040 | bytes 18453340 | solution.py:147
  67.1 1.1 fusion.3
  68.2 1.5 fusion.14
  69.7 0.9 copy-done.13
  70.6 3.5 conditional.5
  71.5 1.1 fusion.27
  72.6 1.5 fusion.38
  75.3 2.1 fusion.153
  77.4 4.4 %conditional.4 = ((f32[8,192]{1,0:T(8,128)S(1)}, f32[8,192]{1,0:T(8,128)S(1)}, f32[8,192,128]{2,1,0:T(8,128)})) conditional(s32[]{:T(128)} %convert_element_type.402, (f32[8,192]{1,0:T(8,128)S(1)}, f32[8,192]{1,0:T(8,128)S(1)}, f32[8,192,128]{2,1,0:T(8,128)}) %tuple.74, (s32[]{:T(128)}, s32[192]{0:T(256)S(1)}, bf16[192,1024]{1,0:T(8,128)(2,1)S(1)}, ...), branch_computations={%region_7.7_spmd, %region_8.10_spmd} | conditional | flops 411799040 | bytes 18453340 | solution.py:147
  78.4 1.1 fusion.3
  79.5 1.4 fusion.14
  81.0 0.9 copy-done.13
  81.9 3.5 conditional.5
  82.8 1.1 fusion.27
  83.9 1.5 fusion.38
  86.6 2.1 fusion.153
  90.0 2.2 fusion.153
  93.5 2.1 fusion.153
  96.9 2.1 fusion.153
  100.3 2.1 fusion.153
  103.7 2.1 fusion.153
  107.1 2.1 fusion.153
  110.5 2.1 fusion.153
  113.9 2.1 fusion.153
  117.3 2.1 fusion.153
  119.5 0.9 copy-done.11
  120.3 1.5 copy.164
  121.8 2.5 copy.163
  124.3 2.4 divide_convert_fusion
  126.7 4.6 %slice.72 = bf16[16,8,128,128]{2,1,3,0:T(8,128)(2,1)} slice(bf16[16,8,128,129]{2,1,3,0:T(8,128)(2,1)} %all-gather.8.cloned.1.call-done), slice={[0:16], [0:8], [0:128], [0:128]} | slice | bytes 8388608 | tf_op jit(solution)/shard_map/slice | solution.py:26
  131.2 6.7 %copy.225 = bf16[16,8,128,128]{3,2,1,0:T(8,128)(2,1)} copy(bf16[16,8,128,128]{2,1,3,0:T(8,128)(2,1)} %slice.72) | data formatting | bytes 8388608
  137.9 3.2 select_reduce_fusion
  142.3 1.1 fusion.100
  144.2 1.1 multiply_reduce_fusion
  145.8 1.2 fusion.69
  147.3 2.8 fusion.128
  150.8 0.9 add_select_fusion
  152.0 0.9 fusion.115
  152.9 1.2 copy-done.2
  154.5 1.7 divide_multiply_fusion
  157.1 0.8 copy.177
  158.5 92.6 %all-gather.1 = bf16[128,128]{1,0:T(8,128)(2,1)S(1)} all-gather(bf16[8,128]{1,0:T(8,128)(2,1)S(1)} %add_convert_fusion), channel_id=3, replica_groups=mesh['seq'=16,'head'=16] {'seq'}, dimensions={0}, use_global_device_ids=true | all-gather | bytes 34816 | tf_op jit(solution)/shard_map/all_gather | solution.py:238
  251.1 4.7 %fusion.117 = f32[8,384,128]{2,1,0:T(8,128)S(1)} fusion(bf16[8,384,128]{2,1,0:T(8,128)(2,1)S(1)} %select_convert_fusion.2, f32[8,384,384]{1,2,0:T(8,128)} %copy-done.2), kind=kOutput, calls=%fused_computation.179 | convolution fusion | flops 306708480 | bytes 7077888 | tf_op jit(solution)/shard_map/hrs,hrf->hsf/dot_general | solution.py:53
  255.9 1.9 fusion.113
  257.8 7.1 %all-gather.12.cloned.1.call-done = bf16[128,128,128]{2,1,0:T(8,128)(2,1)} async-done(((bf16[8,128,128]{2,1,0:T(8,128)(2,1)}), bf16[128,128,128]{2,1,0:T(8,128)(2,1)}) %all-gather.12.cloned.1.call-update) | async-done | bytes 4194320 | tf_op jit(solution)/shard_map/all_gather | solution.py:235
  264.9 3.2 fusion.48
  268.7 1.0 copy-done.7
  269.7 2.1 fusion.55
  274.1 54.6 %all-gather.14.cloned.1.call-done = bf16[4194304]{0:T(1024)(128)(2,1)} async-done(((bf16[262144]{0:T(1024)(128)(2,1)}), bf16[4194304]{0:T(1024)(128)(2,1)}) %all-gather.14.cloned.1.call-update) | async-done | bytes 8388624 | tf_op jit(solution)/shard_map/all_gather | solution.py:35
  328.7 7.6 %reshape.299 = bf16[16,262144]{1,0:T(8,128)(2,1)} reshape(bf16[4194304]{0:T(1024)(128)(2,1)} %all-gather.14.cloned.1.call-done) | data formatting | bytes 16777216 | tf_op jit(solution)/shard_map/all_gather | solution.py:35
  336.4 11.9 %reduce_sum.103 = bf16[262144]{0:T(1024)(128)(2,1)S(1)} reduce(bf16[16,262144]{1,0:T(8,128)(2,1)} %reshape.299, bf16[]{:T(256)} %constant.99.clone.1), dimensions={0}, to_apply=%region_19.20 | reduce | flops 3932160 | bytes 8912898 | tf_op jit(solution)/shard_map/reduce_sum | solution.py:35
  (151 shorter events, 17.0 us)
Async XLA Ops:
  7.2 10.8 %copy-start = (bf16[8,128,128]{2,1,0:T(8,128)(2,1)S(1)}, bf16[8,128,128]{2,1,0:T(8,128)(2,1)}, u32[]{:S(2)}) copy-start(bf16[8,128,128]{2,1,0:T(8,128)(2,1)} %param.15) | copy-start | bytes 786436
  7.2 9.3 %copy-start.5 = (bf16[384,1024]{1,0:T(8,128)(2,1)S(1)}, bf16[384,1024]{1,0:T(8,128)(2,1)}, u32[]{:S(2)}) copy-start(bf16[384,1024]{1,0:T(8,128)(2,1)} %param.11) | copy-start | bytes 2359300
  7.2 54.6 %all-gather.10.cloned.1.call-start = ((), (), s32[]{:S(2)}) async-start(), calls=%async_computation.1 | async-start | bytes 3342336 | tf_op jit(solution)/shard_map/all_gather | solution.py:120
  8.2 8.3 %copy-start.18 = (bf16[8,128,128]{2,1,0:T(8,128)(2,1)S(1)}, bf16[8,128,128]{2,1,0:T(8,128)(2,1)}, u32[]{:S(2)}) copy-start(bf16[8,128,128]{2,1,0:T(8,128)(2,1)} %param.14) | copy-start | bytes 786436
  9.3 5.5 %collective-permute-start = (bf16[2,384,64]{2,1,0:T(8,128)(2,1)S(1)}, bf16[2,384,64]{2,1,0:T(8,128)(2,1)S(1)}, u32[]{:S(2)}, u32[]{:S(2)}) collective-permute-start(bf16[2,384,64]{2,1,0:T(8,128)(2,1)S(1)} %pad_maximum_fusion.3), channel_id=1, source_target_pairs={{0,1},{1,0},{2,3},{3,2},{4,5},{5,4},{6,7},{7,6},{8,9},{9,8},{10,11... | collective-permute-start | bytes 294920 | tf_op jit(solution)/shard_map/ppermute | solution.py:18
  15.7 111.0 %all-gather.8.cloned.1.call-start = ((), (), s32[]{:S(2)}) async-start(), calls=%async_computation | async-start | bytes 4491264 | tf_op jit(solution)/shard_map/all_gather | solution.py:24
  17.0 2.2 copy-start.3
  17.0 1.1 copy-start.8
  19.2 1.2 copy-start.14
  19.2 2.2 copy-start.9
  21.2 243.7 %all-gather.12.cloned.1.call-start = ((), (), s32[]{:S(2)}) async-start(), calls=%async_computation.2 | async-start | bytes 4456448 | tf_op jit(solution)/shard_map/all_gather | solution.py:235
  67.1 1.1 copy-start.12
  69.7 0.9 copy-start.13
  78.4 1.2 copy-start.12
  81.0 0.9 copy-start.13
  119.5 0.9 copy-start.11
  141.8 2.4 copy-start.19
  142.2 1.9 copy-start.16
  142.3 1.9 copy-start.17
  147.0 181.7 %all-gather.14.cloned.1.call-start = ((), (), s32[]{:S(2)}) async-start(), calls=%async_computation.3 | async-start | bytes 8912896 | tf_op jit(solution)/shard_map/all_gather | solution.py:35
  150.8 1.1 copy-start.10
  152.0 2.1 copy-start.2
  152.0 2.5 copy-start.4
  154.5 1.7 copy-start.6
  156.2 99.7 %slice-start = ((s8[4718592]{0:T(1024)(128)(4,1)}), s8[524288]{0:T(1024)(128)(4,1)S(1)}, s32[]{:S(2)}) async-start(s8[4718592]{0:T(1024)(128)(4,1)} %bitcast.271), calls=%async_computation.4 | async-start | bytes 1048576
  158.2 97.7 %slice-start.1 = ((s8[4718592]{0:T(1024)(128)(4,1)}), s8[4194304]{0:T(1024)(128)(4,1)S(1)}, s32[]{:S(2)}) async-start(s8[4718592]{0:T(1024)(128)(4,1)} %bitcast.271), calls=%async_computation.5 | async-start | bytes 8388608
  268.3 1.4 copy-start.7
  272.3 1.0 copy-start.15
  336.4 13.7 %copy-start.1 = (bf16[8,128,128]{2,1,0:T(8,128)(2,1)S(1)}, bf16[8,128,128]{2,1,0:T(8,128)(2,1)}, u32[]{:S(2)}) copy-start(bf16[8,128,128]{2,1,0:T(8,128)(2,1)} %param.15) | copy-start | bytes 786436
Sparse Core Ops, SparseCore 0:
  15.8 45.9 all-gather.9
  63.7 40.6 all-gather.7
  147.1 117.7 all-gather.11
  274.2 54.4 all-gather.13
